TPU v7x, 512 devices: a whole 4x4x16 slice. The times are simulated.
512 devices in a mesh: req: 64 (over z, y), hid: 8 (over x, core).
Axes of the slice: x: 4, y: 4, z: 16, core: 2. Of those that a mesh axis runs over, the one named last changes fastest.
Arguments:
- resid: bfloat16 [8192, 1024], P('req'), may hold values from -6 to 6
- attn_gain: float32 [1024], replicated, may hold values from 0.25 to 1.75
- w_query: bfloat16 [1024, 1024], P(None, 'hid'), may hold values from -4 to 4
- w_key: bfloat16 [1024, 1024], P(None, 'hid'), may hold values from -1 to 1
- w_value: bfloat16 [1024, 1024], P(None, 'hid'), may hold values from -0.1875 to 0.1875
- w_attn_out: bfloat16 [1024, 1024], P('hid'), may hold values from -0.1875 to 0.1875
- cache: bfloat16 [2048, 2, 16, 1024], P('req', None, None, 'hid'), may hold values from -48 to 48
- cache_lens: int32 [2048], P('req'), may hold values from 1 to 16
- seg_ids: int32 [64, 96], P('req'), may hold values from 0 to 3, never falling along the last dimension, each value on 1 to 48 neighbouring positions
- ffn_gain: float32 [1024], replicated, may hold values from 0.25 to 1.75
- router: bfloat16 [1024, 16], replicated, may hold values from -0.078125 to 0.078125
- routes: int32 [8192, 2], P('req'), may hold values from 0 to 15, all different within a row; in each aligned block of 16 rows (0 to 15, 16 to 31, ...) at most 3 rows name the same one
- w_in: bfloat16 [2, 1024, 45056], P(None, None, ('req', 'hid')), may hold values from -0.1875 to 0.1875
- w_out: bfloat16 [45056, 1024], P('req'), may hold values from -0.109375 to 0.109375
Outputs:
- layer_out: bfloat16 [8192, 1024], P(('req', 'hid'))
Inputs may be any that keep to these rules, and one draw needn't show every extreme that they name: `routes`: in every aligned block of 16 rows no expert is named more than 3 times, so no assignment is dropped.
All inputs are finite; a program needn't handle non-finite values.
Results may differ from a plain program's by a relative error of at most 0.012.
The roundings to bfloat16 on the way count: a program that leaves them out, or rounds other values in their place, can miss the bound.
Values may be sent and summed in bfloat16 or wider, within the bound.
No kernel may reach another device: no remote copies, remote signals or barrier semaphores. Data moves between devices by JAX's collectives and lax.ppermute only.
A program may use at most 64 MiB of HBM per device.

v0:
```python
import jax
import jax.numpy as jnp
from jax import lax
from jax.sharding import PartitionSpec as P

HDIM = 64
EPS = 1e-06


def rms_scale(values, gain):
    values = values.astype(jnp.float32)
    inverse = lax.rsqrt(jnp.mean(values * values, axis=-1, keepdims=True) + EPS)
    return (values * inverse * gain).astype(jnp.bfloat16)


def softmax_bf16(scores, allowed):
    scores = jnp.where(allowed, scores, -jnp.inf)
    highest = jnp.max(scores, axis=-1, keepdims=True)
    weights = jnp.exp(scores - highest)
    return (weights / jnp.sum(weights, axis=-1, keepdims=True)).astype(jnp.bfloat16)


def attend(normed, w_query, w_key, w_value, segments, cached, lengths):
    heads = w_query.shape[1] // HDIM
    scale = HDIM ** (-0.5)
    total = normed.shape[0]
    packed = segments.shape[0]
    decoded = total - packed
    slots = cached.shape[2]
    query = (
        jnp.dot(normed, w_query, preferred_element_type=jnp.float32)
        .astype(jnp.bfloat16)
        .reshape(total, heads, HDIM)
    )
    keys = (
        jnp.dot(normed, w_key, preferred_element_type=jnp.float32)
        .astype(jnp.bfloat16)
        .reshape(total, heads, HDIM)
    )
    values = (
        jnp.dot(normed, w_value, preferred_element_type=jnp.float32)
        .astype(jnp.bfloat16)
        .reshape(total, heads, HDIM)
    )
    positions = jnp.arange(packed)
    allowed = (positions[None, :] <= positions[:, None]) & (segments[None, :] == segments[:, None])
    scores = (
        jnp.einsum(
            "qhd,khd->hqk", query[:packed], keys[:packed], preferred_element_type=jnp.float32
        )
        * scale
    )
    weights = softmax_bf16(scores, allowed[None])
    prompt_ctx = jnp.einsum(
        "hqk,khd->qhd", weights, values[:packed], preferred_element_type=jnp.float32
    )
    stored = cached.reshape(decoded, 2, slots, heads, HDIM)
    cached_scores = (
        jnp.einsum(
            "uhd,uchd->uhc", query[packed:], stored[:, 0], preferred_element_type=jnp.float32
        )
        * scale
    )
    own_scores = (
        jnp.sum(
            query[packed:].astype(jnp.float32) * keys[packed:].astype(jnp.float32),
            axis=-1,
            keepdims=True,
        )
        * scale
    )
    valid = jnp.arange(slots)[None, None, :] < lengths[:, None, None]
    allowed_all = jnp.concatenate(
        [jnp.broadcast_to(valid, cached_scores.shape), jnp.ones(own_scores.shape, dtype=bool)],
        axis=-1,
    )
    joined = jnp.concatenate([cached_scores, own_scores], axis=-1)
    weights_dec = softmax_bf16(joined, allowed_all)
    decode_ctx = jnp.einsum(
        "uhc,uchd->uhd", weights_dec[..., :slots], stored[:, 1], preferred_element_type=jnp.float32
    )
    decode_ctx = decode_ctx + weights_dec[..., slots:].astype(jnp.float32) * values[packed:].astype(
        jnp.float32
    )
    context = jnp.concatenate([prompt_ctx, decode_ctx], axis=0)
    return context.reshape(total, heads * HDIM).astype(jnp.bfloat16)


def route_block(chosen, gate_logits, capacity):
    count = chosen.shape[0]
    experts = gate_logits.shape[1]
    flat = chosen.reshape(count * 2)
    onehot = (flat[:, None] == jnp.arange(experts, dtype=jnp.int32)[None, :]).astype(jnp.int32)
    earlier = jnp.cumsum(onehot, axis=0) - onehot
    slot = jnp.sum(earlier * onehot, axis=1)
    target = flat * capacity + slot
    placed = (target[:, None] == jnp.arange(experts * capacity, dtype=jnp.int32)[None, :]).astype(
        jnp.float32
    )
    placed = placed.reshape(count, 2, experts * capacity)
    picked_logits = jnp.sum(
        onehot.reshape(count, 2, experts).astype(jnp.float32) * gate_logits[:, None, :], axis=-1
    )
    gates = jax.nn.sigmoid(picked_logits)
    dispatch = jnp.sum(placed, axis=1).astype(jnp.bfloat16)
    combine_w = jnp.sum(placed * gates[:, :, None], axis=1)
    return (dispatch, combine_w)


def hidden_units(tokens_in, w_in):
    gate_val = jnp.dot(tokens_in, w_in[0], preferred_element_type=jnp.float32)
    up_val = jnp.dot(tokens_in, w_in[1], preferred_element_type=jnp.float32)
    return (jax.nn.gelu(gate_val, approximate=True) * up_val).astype(jnp.bfloat16)


def body(
    resid,
    attn_gain,
    w_query,
    w_key,
    w_value,
    w_attn_out,
    cache,
    cache_lens,
    seg_ids,
    ffn_gain,
    router,
    routes,
    w_in,
    w_out,
):
    req_count = lax.axis_size("req")
    hid_count = lax.axis_size("hid")
    hid_index = lax.axis_index("hid")
    experts = router.shape[1]
    replicas = req_count // experts
    group_rows = resid.shape[0]
    block_rows = group_rows // hid_count
    capacity = max(2, (5 * block_rows + 31) // 32)
    width = resid.shape[1]
    row_start = hid_index * block_rows
    normed = rms_scale(resid, attn_gain)
    context = attend(normed, w_query, w_key, w_value, seg_ids[0], cache, cache_lens)
    partial_mix = jnp.dot(context, w_attn_out, preferred_element_type=jnp.float32)
    mixed = lax.psum(partial_mix, "hid")
    after = resid.astype(jnp.float32) + mixed
    full_ffn = rms_scale(after, ffn_gain)
    own_after = lax.dynamic_slice_in_dim(after, row_start, block_rows, 0)
    logits = jnp.dot(full_ffn, router, preferred_element_type=jnp.float32)
    all_routes = routes.reshape(hid_count, block_rows, 2)
    all_logits = logits.reshape(hid_count, block_rows, experts)
    dispatch_all, combine_all = jax.vmap(
        lambda chosen, gate_logits: route_block(chosen, gate_logits, capacity)
    )(all_routes, all_logits)
    combine_w = lax.dynamic_index_in_dim(combine_all, hid_index, 0, keepdims=False)
    all_tokens = full_ffn.reshape(hid_count, block_rows, width)
    outgoing = jnp.einsum(
        "nbs,nbd->nsd", dispatch_all, all_tokens, preferred_element_type=jnp.float32
    ).astype(jnp.bfloat16)
    outgoing = jnp.broadcast_to(
        outgoing.reshape(hid_count, experts, 1, capacity, width),
        (hid_count, experts, replicas, capacity, width),
    )
    outgoing = outgoing.reshape(hid_count, req_count, capacity, width)
    received = lax.all_to_all(outgoing, "req", split_axis=1, concat_axis=1, tiled=True)
    hidden = hidden_units(received.reshape(hid_count * req_count * capacity, width), w_in)
    stacked = hidden.reshape(hid_count, req_count * capacity, hidden.shape[1])
    projected = jnp.dot(
        lax.all_to_all(stacked, "hid", split_axis=0, concat_axis=2, tiled=True)[0],
        w_out,
        preferred_element_type=jnp.float32,
    ).astype(jnp.bfloat16)[None]
    returned = lax.all_to_all(
        projected.reshape(req_count * capacity, width),
        "req",
        split_axis=0,
        concat_axis=0,
        tiled=True,
    )
    summed = jnp.sum(
        returned.astype(jnp.float32).reshape(experts, replicas, capacity, width), axis=1
    )
    ffn_total = jnp.dot(
        combine_w,
        summed.reshape(experts * capacity, width),
        precision=lax.Precision.HIGHEST,
        preferred_element_type=jnp.float32,
    )
    return (own_after + ffn_total).astype(jnp.bfloat16)


def solution(mesh):
    in_specs = (
        P("req", None),
        P(),
        P(None, "hid"),
        P(None, "hid"),
        P(None, "hid"),
        P("hid", None),
        P("req", None, None, "hid"),
        P("req"),
        P("req", None),
        P(),
        P(),
        P("req", None),
        P(None, None, ("req", "hid")),
        P("req", None),
    )
    out_specs = P(("req", "hid"), None)
    return jax.shard_map(body, mesh=mesh, in_specs=in_specs, out_specs=out_specs, check_vma=False)
```

profile of v0, /device:TPU:8, one launch (start us, length us, event | category | flops | bytes accessed | tf_op | source)
XLA Modules:
  0.0 338.4 jit_solution(14188825207988231362)
XLA Ops:
  6.5 0.0 copy-start
  6.6 0.0 all-reduce.3.cloned.1.call-start
  6.6 1.2 fusion.15
  7.8 1.3 convolution_convert_fusion.4
  9.2 0.0 copy-start.3
  9.2 0.1 slice.58
  9.3 0.1 reshape.189
  9.4 1.3 convolution_convert_fusion.3
  10.7 0.1 reshape.180
  10.8 0.1 multiply_reduce_fusion.3
  10.9 0.1 copy.114
  11.0 1.2 reshape.174
  12.2 0.2 slice_bitcast_fusion.1
  12.4 0.2 fusion.18
  12.7 0.1 copy.103
  12.8 0.0 copy-done.9
  12.8 0.0 copy-start.6
  13.0 0.1 copy.83
  13.1 0.1 copy.84
  13.2 0.0 copy-done.8
  13.2 0.1 fusion.27
  13.3 0.2 fusion.5
  13.5 0.3 fusion.44
  13.8 0.0 copy-start.5
  13.8 0.3 convolution_convert_fusion.5
  14.2 0.2 copy.113
  14.4 0.7 multiply_reduce_fusion
  15.1 0.1 copy.109
  15.2 0.1 copy.110
  15.3 0.1 copy.82
  15.4 0.2 fusion.7
  15.6 0.1 pad_maximum_fusion
  15.7 1.1 fusion.46
  16.8 0.0 all-reduce.3.cloned.1.call-update
  16.8 0.1 copy.88
  16.9 0.1 eq.58
  17.0 0.1 copy.89
  17.1 0.7 fusion.45
  17.8 0.1 reshape_reshape.4
  17.9 0.1 copy.90
  18.0 79.3 %all-reduce.3.cloned.1.call-done = f32[128,1024]{1,0:T(8,128)} async-done(((f32[128,1024]{1,0:T(8,128)}), f32[128,1024]{1,0:T(8,128)}) %all-reduce.3.cloned.1.call-update) | async-done | bytes 524304 | tf_op jit(solution)/shard_map/psum | solution.py:145
  97.3 1.2 multiply_reduce_fusion.1
  98.5 0.1 multiply_convert_fusion
  98.7 0.2 fusion.47
  98.9 0.2 multiply_reduce_fusion.2
  99.1 0.1 select_reduce_fusion
  99.3 0.4 convolution_convert_fusion
  99.7 0.4 copy.96
  100.1 0.4 broadcast_in_dim.27
  100.5 158.6 %all_to_all.29 = bf16[8,64,3,1024]{3,0,2,1:T(8,128)(2,1)S(1)} all-to-all(bf16[8,64,3,1024]{3,0,2,1:T(8,128)(2,1)S(1)} %bitcast.73), channel_id=1, replica_groups=mesh['req'=64,'hid'=8] {'req'}, dimensions={1} | all-to-all | bytes 6291456 | tf_op jit(solution)/shard_map/all_to_all | solution.py:165
  259.1 4.6 %copy.97 = bf16[8,64,3,1024]{3,2,1,0:T(4,128)(2,1)} copy(bf16[8,64,3,1024]{3,0,2,1:T(8,128)(2,1)S(1)} %all_to_all.29) | data formatting | bytes 6291456 | tf_op jit(solution)/shard_map/all_to_all | solution.py:165
  263.7 8.9 %reshape.177 = bf16[1536,1024]{1,0:T(8,128)(2,1)} reshape(bf16[8,64,3,1024]{3,2,1,0:T(4,128)(2,1)} %copy.97) | data formatting | bytes 6291456 | tf_op jit(solution)/shard_map/reshape | solution.py:166
  272.6 3.1 fusion.21
  275.7 1.1 fusion.1
  276.8 0.3 reshape.178
  277.1 0.1 copy.98
  277.2 13.2 %all_to_all.30 = bf16[8,192,88]{1,2,0:T(8,128)(2,1)S(1)} all-to-all(bf16[8,192,88]{1,2,0:T(8,128)(2,1)S(1)} %copy.98), channel_id=1, replica_groups=mesh['req'=64,'hid'=8] {'hid'}, dimensions={0} | all-to-all | bytes 540672 | tf_op jit(solution)/shard_map/all_to_all | solution.py:169
  290.3 0.5 convolution_convert_fusion.1
  290.9 1.0 all_to_all.24
  291.9 5.9 %all-to-all-start.2 = ((bf16[64,3,1024]{2,1,0:T(4,128)(2,1)}), bf16[64,3,1024]{2,1,0:T(4,128)(2,1)S(1)}, u32[]{:S(2)}, u32[]{:S(2)}) async-start(bf16[64,3,1024]{2,1,0:T(4,128)(2,1)} %all_to_all.24), calls=%async_computation.2 | async-start | bytes 1048576 | tf_op jit(solution)/shard_map/all_to_all | solution.py:173
  297.8 32.6 %all-to-all-done.2 = bf16[64,3,1024]{2,1,0:T(4,128)(2,1)S(1)} async-done(((bf16[64,3,1024]{2,1,0:T(4,128)(2,1)}), bf16[64,3,1024]{2,1,0:T(4,128)(2,1)S(1)}, u32[]{:S(2)}, u32[]{:S(2)}) %all-to-all-start.2) | async-done | bytes 393248 | tf_op jit(solution)/shard_map/all_to_all | solution.py:173
  330.4 0.2 convert_reduce_fusion
  330.6 0.1 reshape.179
  330.8 0.8 fusion.6
  (41 shorter events, 0.3 us)
Async XLA Ops:
  6.5 283.8 %copy-start = (bf16[704,1024]{1,0:T(8,128)(2,1)S(1)}, bf16[704,1024]{1,0:T(8,128)(2,1)}, u32[]{:S(2)}) copy-start(bf16[704,1024]{1,0:T(8,128)(2,1)} %param.27) | copy-start | bytes 4325380
  6.5 7.3 %copy-start.2 = (bf16[128,1024]{1,0:T(8,128)(2,1)S(1)}, bf16[128,1024]{1,0:T(8,128)(2,1)}, u32[]{:S(2)}) copy-start(bf16[128,1024]{1,0:T(8,128)(2,1)} %param.14) | copy-start | bytes 786436
  6.5 7.3 %copy-start.11 = (f32[1024]{0:T(1024)S(1)}, f32[1024]{0:T(1024)}, u32[]{:S(2)}) copy-start(f32[1024]{0:T(1024)} %param.15) | copy-start | bytes 12292
  6.5 6.2 %copy-start.9 = (s32[32]{0:T(128)S(1)}, s32[32]{0:T(128)}, u32[]{:S(2)}) copy-start(s32[32]{0:T(128)} %param.21) | copy-start | bytes 388
  6.5 6.7 %copy-start.8 = (s32[1,96]{1,0:T(1,128)S(1)}, s32[1,96]{1,0:T(1,128)}, u32[]{:S(2)}) copy-start(s32[1,96]{1,0:T(1,128)} %param.22) | copy-start | bytes 1156
  6.5 7.3 %copy-start.10 = (bf16[1024,128]{1,0:T(8,128)(2,1)S(1)}, bf16[1024,128]{1,0:T(8,128)(2,1)}, u32[]{:S(2)}) copy-start(bf16[1024,128]{1,0:T(8,128)(2,1)} %param.18) | copy-start | bytes 786436
  6.6 90.8 %all-reduce.3.cloned.1.call-start = ((), (), s32[]{:S(2)}) async-start(), calls=%async_computation.3 | async-start | bytes 1048576 | tf_op jit(solution)/shard_map/psum | solution.py:145
  9.2 6.5 %copy-start.3 = (bf16[128,1024]{1,0:T(8,128)(2,1)S(1)}, bf16[128,1024]{1,0:T(8,128)(2,1)}, u32[]{:S(2)}) copy-start(bf16[128,1024]{1,0:T(8,128)(2,1)} %param.19) | copy-start | bytes 786436
  11.0 5.8 %copy-start.7 = (s32[128,2]{0,1:T(2,128)S(1)}, s32[128,2]{0,1:T(2,128)}, u32[]{:S(2)}) copy-start(s32[128,2]{0,1:T(2,128)} %param.25) | copy-start | bytes 3076
  12.8 85.8 %copy-start.6 = (f32[1024]{0:T(1024)S(1)}, f32[1024]{0:T(1024)}, u32[]{:S(2)}) copy-start(f32[1024]{0:T(1024)} %param.23) | copy-start | bytes 12292
  13.8 84.8 %copy-start.5 = (bf16[1024,16]{0,1:T(8,128)(2,1)S(1)}, bf16[1024,16]{0,1:T(8,128)(2,1)}, u32[]{:S(2)}) copy-start(bf16[1024,16]{0,1:T(8,128)(2,1)} %param.24) | copy-start | bytes 98308
  263.7 8.9 %copy-start.4 = (bf16[2,1024,88]{1,2,0:T(8,128)(2,1)S(1)}, bf16[2,1024,88]{1,2,0:T(8,128)(2,1)}, u32[]{:S(2)}) copy-start(bf16[2,1024,88]{1,2,0:T(8,128)(2,1)} %param.26) | copy-start | bytes 1081348
  272.6 3.1 copy-start.1
  291.9 38.5 %all-to-all-start.2 = ((bf16[64,3,1024]{2,1,0:T(4,128)(2,1)}), bf16[64,3,1024]{2,1,0:T(4,128)(2,1)S(1)}, u32[]{:S(2)}, u32[]{:S(2)}) async-start(bf16[64,3,1024]{2,1,0:T(4,128)(2,1)} %all_to_all.24), calls=%async_computation.2 | async-start | bytes 1048576 | tf_op jit(solution)/shard_map/all_to_all | solution.py:173
Sparse Core Ops, SparseCore 0:
  16.9 80.3 all-reduce.2
where the time goes:
time: 339 us; the launch traced here: 338 us
  blocking collectives  172 us (51%)
  waiting for transfers between devices  112 us (33%)
  local copies, waits for them, and re-layouts  18.9 us (6%)
  between operations  13.9 us (4%)
  matrix products  11.1 us (3%)
  starting transfers between devices  5.98 us (2%)
  other arithmetic  5.03 us (1%)
    all_to_all x1, blocking collectives, body(): lax.all_to_all(outgoing, 'req', split_axis=1, concat_axis=1, tiled=True)  159 us
    psum x1, waiting for transfers between devices, body(): mixed = lax.psum(partial_mix, 'hid')  79.3 us
    all_to_all x1, waiting for transfers between devices, body(): lax.all_to_all(projected.reshape(req_count * capacity, width), 'req', spl...  32.6 us
    all_to_all x1, blocking collectives, body(): lax.all_to_all(stacked, 'hid', split_axis=0, concat_axis=2, tiled=True)[0]  13.2 us
    reshape x1, local copies, waits for them, and re-layouts, body(): received.reshape(hid_count * req_count * capacity, width)  8.86 us
  transfers between devices with their start and end apart: 2, of which 2 were waited for; matrix products, arithmetic and copies ran while one was open for 0% of the time, Pallas kernels for 0%

commit v1 on v0

--- a/solution.py
+++ b/solution.py
@@ -142,7 +142,8 @@
     normed = rms_scale(resid, attn_gain)
     context = attend(normed, w_query, w_key, w_value, seg_ids[0], cache, cache_lens)
     partial_mix = jnp.dot(context, w_attn_out, preferred_element_type=jnp.float32)
-    mixed = lax.psum(partial_mix, "hid")
+    match_plate = lambda t0: jnp.sum(lax.all_gather(t0, axis_name="hid"), 0)
+    mixed = match_plate(partial_mix)
     after = resid.astype(jnp.float32) + mixed
     full_ffn = rms_scale(after, ffn_gain)
     own_after = lax.dynamic_slice_in_dim(after, row_start, block_rows, 0)

time: 339 us -> 305 us (0.90)
  waiting for transfers between devices: 112 us -> 75.6 us
    psum x1 -> x0, waiting for transfers between devices: 79.3 us -> none  [body(): mixed = lax.psum(partial_mix, 'hid')]
    all_gather x0 -> x1, waiting for transfers between devices: none -> 43.1 us  [body(): match_plate = lambda t0: jnp.sum(lax.all_gather(t0, axis_name='hid'), 0)]
where the time goes in v1:
time: 305 us; the launch traced here: 304 us
  blocking collectives  172 us (56%)
  waiting for transfers between devices  75.6 us (25%)
  local copies, waits for them, and re-layouts  18.9 us (6%)
  between operations  13.9 us (5%)
  matrix products  11.1 us (4%)
  other arithmetic  6.6 us (2%)
  starting transfers between devices  5.99 us (2%)
    all_to_all x1, blocking collectives, body(): lax.all_to_all(outgoing, 'req', split_axis=1, concat_axis=1, tiled=True)  161 us
    all_gather x1, waiting for transfers between devices, body(): match_plate = lambda t0: jnp.sum(lax.all_gather(t0, axis_name='hid'), 0)  43.1 us
    all_to_all x1, waiting for transfers between devices, body(): lax.all_to_all(projected.reshape(req_count * capacity, width), 'req', spl...  32.5 us
    all_to_all x1, blocking collectives, body(): lax.all_to_all(stacked, 'hid', split_axis=0, concat_axis=2, tiled=True)[0]  11.3 us
    reshape x1, local copies, waits for them, and re-layouts, body(): received.reshape(hid_count * req_count * capacity, width)  8.86 us
  transfers between devices with their start and end apart: 2, of which 2 were waited for; matrix products, arithmetic and copies ran while one was open for 0% of the time, Pallas kernels for 0%

profile of v1, /device:TPU:8, one launch (start us, length us, event | category | flops | bytes accessed | tf_op | source)
XLA Modules:
  0.0 304.4 jit_solution(10762042407331182361)
XLA Ops:
  6.5 0.0 copy-start
  6.6 0.0 all-gather.3.cloned.1.call-start
  6.6 1.2 fusion.15
  7.8 1.3 convolution_convert_fusion.4
  9.2 0.0 copy-start.3
  9.2 0.1 slice.58
  9.3 0.1 reshape.190
  9.4 1.3 convolution_convert_fusion.3
  10.7 0.1 reshape.180
  10.8 0.1 multiply_reduce_fusion.3
  10.9 0.1 copy.114
  11.0 1.2 reshape.174
  12.2 0.2 slice_bitcast_fusion.1
  12.4 0.2 fusion.18
  12.7 0.1 copy.103
  12.8 0.0 copy-done.9
  13.0 0.1 copy.83
  13.1 0.1 copy.84
  13.2 0.1 fusion.27
  13.3 0.2 fusion.5
  13.5 0.3 fusion.44
  13.8 0.0 copy-done.11
  13.8 0.3 convolution_convert_fusion.5
  14.1 0.2 copy.113
  14.3 0.7 multiply_reduce_fusion
  15.1 0.1 copy.109
  15.2 0.1 copy.110
  15.3 0.1 copy.82
  15.4 0.2 fusion.7
  15.6 0.1 pad_maximum_fusion
  15.7 1.0 fusion.46
  16.7 0.0 all-gather.3.cloned.1.call-update
  16.7 0.1 reshape_reshape.4
  16.8 0.1 copy.88
  16.9 0.0 copy-start.6
  17.0 0.1 eq.58
  17.1 0.1 copy.89
  17.1 0.7 fusion.45
  17.9 0.1 copy.90
  18.0 43.1 %all-gather.3.cloned.1.call-done = f32[1024,1024]{1,0:T(8,128)} async-done(((f32[128,1024]{1,0:T(8,128)}), f32[1024,1024]{1,0:T(8,128)}) %all-gather.3.cloned.1.call-update) | async-done | bytes 4194320 | tf_op jit(solution)/shard_map/all_gather | solution.py:145
  61.0 2.6 reduce_sum.105
  63.7 0.2 multiply_reduce_fusion.1
  63.8 0.1 multiply_convert_fusion
  64.0 0.2 fusion.47
  64.2 0.2 multiply_reduce_fusion.2
  64.4 0.1 select_reduce_fusion
  64.6 0.4 convolution_convert_fusion
  65.0 0.4 copy.96
  65.4 0.4 broadcast_in_dim.27
  65.8 161.0 %all_to_all.29 = bf16[8,64,3,1024]{3,0,2,1:T(8,128)(2,1)S(1)} all-to-all(bf16[8,64,3,1024]{3,0,2,1:T(8,128)(2,1)S(1)} %bitcast.74), channel_id=1, replica_groups=mesh['req'=64,'hid'=8] {'req'}, dimensions={1} | all-to-all | bytes 6291456 | tf_op jit(solution)/shard_map/all_to_all | solution.py:166
  226.8 4.6 %copy.97 = bf16[8,64,3,1024]{3,2,1,0:T(4,128)(2,1)} copy(bf16[8,64,3,1024]{3,0,2,1:T(8,128)(2,1)S(1)} %all_to_all.29) | data formatting | bytes 6291456 | tf_op jit(solution)/shard_map/all_to_all | solution.py:166
  231.4 8.9 %reshape.177 = bf16[1536,1024]{1,0:T(8,128)(2,1)} reshape(bf16[8,64,3,1024]{3,2,1,0:T(4,128)(2,1)} %copy.97) | data formatting | bytes 6291456 | tf_op jit(solution)/shard_map/reshape | solution.py:167
  240.3 3.1 %fusion.21 = f32[1536,88]{0,1:T(8,128)S(1)} fusion(bf16[1536,1024]{1,0:T(8,128)(2,1)} %reshape.177, bf16[2,1024,88]{1,2,0:T(8,128)(2,1)S(1)} %copy-done.4), kind=kOutput, calls=%fused_computation.41 | convolution fusion | flops 276824064 | bytes 3866624 | tf_op jit(solution)/shard_map/dot_general | solution.py:111
  243.4 1.1 fusion.1
  244.5 0.3 reshape.178
  244.8 0.1 copy.98
  244.9 11.3 %all_to_all.30 = bf16[8,192,88]{1,2,0:T(8,128)(2,1)S(1)} all-to-all(bf16[8,192,88]{1,2,0:T(8,128)(2,1)S(1)} %copy.98), channel_id=1, replica_groups=mesh['req'=64,'hid'=8] {'hid'}, dimensions={0} | all-to-all | bytes 540672 | tf_op jit(solution)/shard_map/all_to_all | solution.py:170
  256.3 0.5 convolution_convert_fusion.1
  256.8 1.0 all_to_all.24
  257.8 6.0 %all-to-all-start.2 = ((bf16[64,3,1024]{2,1,0:T(4,128)(2,1)}), bf16[64,3,1024]{2,1,0:T(4,128)(2,1)S(1)}, u32[]{:S(2)}, u32[]{:S(2)}) async-start(bf16[64,3,1024]{2,1,0:T(4,128)(2,1)} %all_to_all.24), calls=%async_computation.2 | async-start | bytes 1048576 | tf_op jit(solution)/shard_map/all_to_all | solution.py:174
  263.8 32.5 %all-to-all-done.2 = bf16[64,3,1024]{2,1,0:T(4,128)(2,1)S(1)} async-done(((bf16[64,3,1024]{2,1,0:T(4,128)(2,1)}), bf16[64,3,1024]{2,1,0:T(4,128)(2,1)S(1)}, u32[]{:S(2)}, u32[]{:S(2)}) %all-to-all-start.2) | async-done | bytes 393248 | tf_op jit(solution)/shard_map/all_to_all | solution.py:174
  296.3 0.2 convert_reduce_fusion
  296.6 0.1 reshape.179
  296.7 0.8 fusion.6
  (42 shorter events, 0.3 us)
Async XLA Ops:
  6.5 249.7 %copy-start = (bf16[704,1024]{1,0:T(8,128)(2,1)S(1)}, bf16[704,1024]{1,0:T(8,128)(2,1)}, u32[]{:S(2)}) copy-start(bf16[704,1024]{1,0:T(8,128)(2,1)} %param.27) | copy-start | bytes 4325380
  6.5 7.3 %copy-start.2 = (bf16[128,1024]{1,0:T(8,128)(2,1)S(1)}, bf16[128,1024]{1,0:T(8,128)(2,1)}, u32[]{:S(2)}) copy-start(bf16[128,1024]{1,0:T(8,128)(2,1)} %param.14) | copy-start | bytes 786436
  6.5 7.3 %copy-start.11 = (f32[1024]{0:T(1024)S(1)}, f32[1024]{0:T(1024)}, u32[]{:S(2)}) copy-start(f32[1024]{0:T(1024)} %param.15) | copy-start | bytes 12292
  6.5 6.2 %copy-start.9 = (s32[32]{0:T(128)S(1)}, s32[32]{0:T(128)}, u32[]{:S(2)}) copy-start(s32[32]{0:T(128)} %param.21) | copy-start | bytes 388
  6.5 6.7 %copy-start.8 = (s32[1,96]{1,0:T(1,128)S(1)}, s32[1,96]{1,0:T(1,128)}, u32[]{:S(2)}) copy-start(s32[1,96]{1,0:T(1,128)} %param.22) | copy-start | bytes 1156
  6.5 7.3 %copy-start.10 = (bf16[1024,128]{1,0:T(8,128)(2,1)S(1)}, bf16[1024,128]{1,0:T(8,128)(2,1)}, u32[]{:S(2)}) copy-start(bf16[1024,128]{1,0:T(8,128)(2,1)} %param.18) | copy-start | bytes 786436
  6.6 54.5 %all-gather.3.cloned.1.call-start = ((), (), s32[]{:S(2)}) async-start(), calls=%async_computation.3 | async-start | bytes 4718592 | tf_op jit(solution)/shard_map/all_gather | solution.py:145
  9.2 6.5 %copy-start.3 = (bf16[128,1024]{1,0:T(8,128)(2,1)S(1)}, bf16[128,1024]{1,0:T(8,128)(2,1)}, u32[]{:S(2)}) copy-start(bf16[128,1024]{1,0:T(8,128)(2,1)} %param.19) | copy-start | bytes 786436
  11.0 5.7 %copy-start.7 = (s32[128,2]{0,1:T(2,128)S(1)}, s32[128,2]{0,1:T(2,128)}, u32[]{:S(2)}) copy-start(s32[128,2]{0,1:T(2,128)} %param.25) | copy-start | bytes 3076
  16.9 46.9 %copy-start.6 = (f32[1024]{0:T(1024)S(1)}, f32[1024]{0:T(1024)}, u32[]{:S(2)}) copy-start(f32[1024]{0:T(1024)} %param.23) | copy-start | bytes 12292
  61.0 2.9 copy-start.5
  231.4 8.9 %copy-start.4 = (bf16[2,1024,88]{1,2,0:T(8,128)(2,1)S(1)}, bf16[2,1024,88]{1,2,0:T(8,128)(2,1)}, u32[]{:S(2)}) copy-start(bf16[2,1024,88]{1,2,0:T(8,128)(2,1)} %param.26) | copy-start | bytes 1081348
  240.3 3.1 %copy-start.1 = (bf16[1536,1024]{1,0:T(8,128)(2,1)S(1)}, bf16[1536,1024]{1,0:T(8,128)(2,1)}, u32[]{:S(2)}) copy-start(bf16[1536,1024]{1,0:T(8,128)(2,1)} %reshape.177) | copy-start | bytes 9437188
  257.8 38.5 %all-to-all-start.2 = ((bf16[64,3,1024]{2,1,0:T(4,128)(2,1)}), bf16[64,3,1024]{2,1,0:T(4,128)(2,1)S(1)}, u32[]{:S(2)}, u32[]{:S(2)}) async-start(bf16[64,3,1024]{2,1,0:T(4,128)(2,1)} %all_to_all.24), calls=%async_computation.2 | async-start | bytes 1048576 | tf_op jit(solution)/shard_map/all_to_all | solution.py:174
Sparse Core Ops, SparseCore 0:
  16.9 44.1 all-gather.2
